TPU v7x, 512 devices: a whole 4x8x8 slice. The times are simulated.
512 devices in a mesh: frame: 16 (over x, y_lo, core), crop: 4 (over y_hi), dp: 8 (over z).
Axes of the slice: x: 4, y: 8 (y_hi: 4, y_lo: 2; y = y_hi * 2 + y_lo), z: 8, core: 2. Of those that a mesh axis runs over, the one named last changes fastest.
Arguments:
- global_clips: bfloat16 [8, 16, 256, 1408], P('dp', 'frame', 'crop'), may hold values from -6 to 6
- frame_map: int32 [8, 16, 8], P('dp', 'crop'), may hold values from 0 to 15
- teacher_qkv: bfloat16 [1408, 4224], P(None, 'frame'), may hold values from -0.15625 to 0.15625
- teacher_out: bfloat16 [1408, 1408], P('frame'), may hold values from -0.15625 to 0.15625
- teacher_bottle: bfloat16 [1408, 256], replicated, may hold values from -0.15625 to 0.15625
- student_qkv: bfloat16 [1408, 4224], P(None, 'frame'), may hold values from -0.15625 to 0.15625
- student_out: bfloat16 [1408, 1408], P('frame'), may hold values from -0.15625 to 0.15625
- student_bottle: bfloat16 [1408, 256], replicated, may hold values from -0.15625 to 0.15625
- prototypes: bfloat16 [256, 32768], P(None, 'frame'), may hold values from -1.796875 to 1.796875
- center: float32 [32768], P('frame'), may hold values from -8.6 to -3.9
Outputs:
- grad_qkv: float32 [1408, 4224], P(('crop', 'dp'), 'frame')
- grad_out: float32 [1408, 1408], P('frame', ('crop', 'dp'))
- grad_bottle: float32 [1408, 256], P(('crop', 'dp'))
All inputs are finite; a program needn't handle non-finite values.
Results may differ from a plain program's by a relative error of at most 0.00035.
Values may be sent and summed in bfloat16 or wider, within the bound.
No kernel may reach another device: no remote copies, remote signals or barrier semaphores. Data moves between devices by JAX's collectives and lax.ppermute only.
A program may use at most 64 MiB of HBM per device.

v0:
```python
import math
import jax
import jax.numpy as jnp
from jax import lax
from jax.sharding import PartitionSpec as P

D = 1408
HEADS = 16
HIGH = lax.Precision.HIGHEST
TAU_TEACH = 0.04
TAU_STUD = 0.1


def combined_all(value, axis, join):
    pieces = jax.tree.map(lambda part: lax.all_gather(part, axis), value)
    head = jax.tree.map(lambda part: part[0], pieces)
    tail = jax.tree.map(lambda part: part[1:], pieces)
    running, _ = lax.scan(lambda running, share: (join(running, share), None), head, tail)
    return running


def norm_tokens(tokens):
    values = tokens.astype(jnp.float32)
    middle = jnp.mean(values, axis=-1, keepdims=True)
    spread = jnp.mean(jnp.square(values - middle), axis=-1, keepdims=True)
    return ((values - middle) * lax.rsqrt(spread + 1e-06)).astype(jnp.bfloat16)


def attend_core(qkv):
    rounded = lax.optimization_barrier(qkv.astype(jnp.bfloat16)).astype(jnp.float32)
    query = rounded[:, :, :, 0]
    keys = rounded[:, :, :, 1]
    values = rounded[:, :, :, 2]
    scale = 1.0 / math.sqrt(qkv.shape[-1])
    scores = jnp.einsum("iphe,jphe->phij", query, keys, precision=HIGH) * scale
    weights = jax.nn.softmax(scores, axis=-1)
    weights = lax.optimization_barrier(weights.astype(jnp.bfloat16)).astype(jnp.float32)
    return jnp.einsum("phij,jphe->iphe", weights, values, precision=HIGH)


def project(normed, weight, heads_here):
    qkv = jnp.einsum("fpd,dc->fpc", normed, weight, preferred_element_type=jnp.float32)
    return qkv.reshape(normed.shape[0], normed.shape[1], heads_here, 3, -1)


def unit(vector):
    return vector * lax.rsqrt(jnp.sum(vector * vector, axis=-1, keepdims=True) + 1e-06)


def merge_pair(top_a, sum_a, vec_a, top_b, sum_b, vec_b):
    top = jnp.maximum(top_a, top_b)
    factor_a = jnp.exp(top_a - top)
    factor_b = jnp.exp(top_b - top)
    return (
        top,
        sum_a * factor_a + sum_b * factor_b,
        vec_a * factor_a[..., None] + vec_b * factor_b[..., None],
    )


def combine_totals(first, second):
    student = merge_pair(first[0], first[1], first[2], second[0], second[1], second[2])
    teacher = merge_pair(first[3], first[4], first[5], second[3], second[4], second[5])
    return (student[0], student[1], student[2], teacher[0], teacher[1], teacher[2])


def local(
    global_clips,
    frame_map,
    teacher_qkv,
    teacher_out,
    teacher_bottle,
    student_qkv,
    student_out,
    student_bottle,
    prototypes,
    center,
):
    head_size = D // HEADS
    heads_here = teacher_out.shape[0] // head_size
    tokens = global_clips[0]
    gathered = lax.all_gather(tokens, "frame", axis=0, tiled=True)
    frames_all, patches_here = (gathered.shape[0], gathered.shape[1])
    normed = norm_tokens(gathered)
    teacher_count = frames_all * patches_here * lax.axis_size("crop")
    t_att = attend_core(project(normed, teacher_qkv, heads_here))
    t_heads = jnp.sum(t_att, axis=(0, 1)).reshape(-1)
    t_out32 = teacher_out.astype(jnp.float32)
    t_partial = (
        jnp.sum(tokens, axis=(0, 1), dtype=jnp.float32) + jnp.dot(t_heads, t_out32, precision=HIGH)
    ) / teacher_count
    maps = frame_map[0]
    clips_here, local_frames = maps.shape
    order = maps.T.reshape(-1)
    frame_qkv = jnp.einsum(
        "fpd,dc->fpc", normed, student_qkv, preferred_element_type=jnp.float32
    ).astype(jnp.bfloat16)
    picked = jnp.take(frame_qkv, order, axis=0)
    s_qkv = picked.reshape(local_frames, clips_here * patches_here, heads_here, 3, -1)
    s_att = attend_core(s_qkv)
    local_count = local_frames * patches_here
    s_heads = (
        jnp.sum(s_att.reshape(local_frames, clips_here, patches_here, -1), axis=(0, 2))
        / local_count
    )
    s_out32 = student_out.astype(jnp.float32)
    s_partial = jnp.dot(s_heads, s_out32, precision=HIGH)
    frame_sums = jnp.sum(gathered, axis=1, dtype=jnp.float32)
    picks = jnp.sum(
        (maps[:, :, None] == jnp.arange(frames_all, dtype=jnp.int32)[None, None, :]).astype(
            jnp.float32
        ),
        axis=1,
    )
    local_mean = jnp.dot(picks, frame_sums, precision=HIGH) / local_count
    t_pooled = lax.psum(t_partial, ("frame", "crop"))
    s_summed = lax.psum(s_partial, "frame")
    s_pooled = local_mean + s_summed
    protos = prototypes.astype(jnp.float32)
    s_bottle32 = student_bottle.astype(jnp.float32)
    unit_t = unit(jnp.dot(t_pooled, teacher_bottle.astype(jnp.float32), precision=HIGH))
    s_z = jnp.dot(s_pooled, s_bottle32, precision=HIGH)
    unit_s = unit(s_z)
    t_logits = (jnp.dot(unit_t, protos, precision=HIGH) - center) / TAU_TEACH
    s_logits = jnp.dot(unit_s, protos, precision=HIGH) / TAU_STUD
    t_top = jnp.max(t_logits)
    t_exp = jnp.exp(t_logits - t_top)
    s_top = jnp.max(s_logits, axis=-1)
    s_exp = jnp.exp(s_logits - s_top[:, None])
    merged = combined_all(
        (
            s_top,
            jnp.sum(s_exp, axis=-1),
            jnp.dot(s_exp, protos.T, precision=HIGH),
            t_top,
            jnp.sum(t_exp),
            jnp.dot(protos, t_exp, precision=HIGH),
        ),
        "frame",
        combine_totals,
    )
    s_expect = merged[2] / merged[1][:, None]
    t_expect = merged[5] / merged[4]
    all_clips = clips_here * lax.axis_size("crop")
    d_unit = (s_expect - t_expect[None, :]) / (all_clips * TAU_STUD)
    inverse = lax.rsqrt(jnp.sum(s_z * s_z, axis=-1, keepdims=True) + 1e-06)
    d_z = (d_unit - unit_s * jnp.sum(unit_s * d_unit, axis=-1, keepdims=True)) * inverse
    g_bottle = jnp.dot(s_pooled.T, d_z, precision=HIGH)
    d_pooled = jnp.dot(d_z, s_bottle32.T, precision=HIGH)
    g_out = jnp.dot(s_heads.T, d_pooled, precision=HIGH)
    d_heads = jnp.dot(d_pooled, s_out32.T, precision=HIGH) / local_count
    d_att = jnp.broadcast_to(
        d_heads[None, :, None, :], (local_frames, clips_here, patches_here, d_heads.shape[1])
    ).reshape(s_att.shape)
    _, core_back = jax.vjp(attend_core, s_qkv)
    d_qkv = core_back(d_att)[0].reshape(local_frames * clips_here, patches_here, -1)
    selector = (order[:, None] == jnp.arange(frames_all, dtype=jnp.int32)[None, :]).astype(
        jnp.bfloat16
    )
    d_frames = jnp.einsum("rf,rpc->fpc", selector, d_qkv, preferred_element_type=jnp.float32)
    g_qkv = jnp.einsum("fpd,fpc->dc", normed.astype(jnp.float32), d_frames, precision=HIGH)
    summed = (
        lax.psum_scatter(g_qkv, ("crop", "dp"), scatter_dimension=0, tiled=True),
        lax.psum_scatter(g_out, ("crop", "dp"), scatter_dimension=1, tiled=True),
        lax.psum_scatter(g_bottle, ("crop", "dp"), scatter_dimension=0, tiled=True),
    )
    return (summed[0], summed[1], summed[2])


def solution(mesh):
    return jax.shard_map(
        local,
        mesh=mesh,
        in_specs=(
            P("dp", "frame", "crop", None),
            P("dp", "crop", None),
            P(None, "frame"),
            P("frame", None),
            P(),
            P(None, "frame"),
            P("frame", None),
            P(),
            P(None, "frame"),
            P("frame"),
        ),
        out_specs=(P(("crop", "dp"), "frame"), P("frame", ("crop", "dp")), P(("crop", "dp"), None)),
        check_vma=False,
    )
```

profile of v0, /device:TPU:26, one launch (start us, length us, event | category | flops | bytes accessed | tf_op | source)
XLA Modules:
  0.0 642.9 jit_solution(15766449092448168126)
XLA Ops:
  9.4 1.3 dynamic-slice
  12.2 1.6 convert_reduce_fusion.2
  14.4 39.3 %all-gather.9.cloned.1.call-done = bf16[16,1,64,1408]{3,2,1,0:T(8,128)(2,1)} async-done(((bf16[1,1,64,1408]{3,2,1,0:T(8,128)(2,1)}), bf16[16,1,64,1408]{3,2,1,0:T(8,128)(2,1)}) %all-gather.9.cloned.1.call-update) | async-done | bytes 2883600 | tf_op jit(solution)/shard_map/all_gather | solution.py:82
  53.7 3.4 convert_reduce_fusion
  58.6 1.9 fusion.26
  60.5 1.9 gather_fusion
  62.4 4.5 reshape.311
  67.0 1.3 copy_select_fusion
  68.8 6.9 %fusion.83 = (f32[256,8]{1,0:T(8,128)S(1)}, f32[256,8,8]{1,2,0:T(8,128)S(1)}) fusion(f32[256,8,8]{1,2,0:T(8,128)S(1)} %convolution_multiply_fusion.2), kind=kOutput, calls=%fused_computation.133 | output fusion | flops 32775 | bytes 139264 | tf_op jit(solution)/shard_map/sub | solution.py:36
  76.9 45.0 %psum.14 = f32[4,1408]{1,0:T(4,128)S(1)} all-reduce(f32[4,1408]{1,0:T(4,128)S(1)} %fusion.67), channel_id=1, replica_groups=mesh['frame'=16,'crop'=4,'dp'=8] {'frame'}, use_global_device_ids=true, to_apply=%region_8.9 | all-reduce | flops 5632 | bytes 45056 | tf_op jit(solution)/shard_map/psum | solution.py:117
  125.0 25.2 %all-gather.5 = f32[16,4,256]{2,1,0:T(4,128)S(1)} all-gather(f32[1,4,256]{2,1,0:T(4,128)S(1)} %convolution_bitcast_fusion.5), channel_id=5, replica_groups=mesh['frame'=16,'crop'=4,'dp'=8] {'frame'}, dimensions={0}, use_global_device_ids=true | all-gather | bytes 69632 | tf_op jit(solution)/shard_map/all_gather | solution.py:15
  150.9 3.9 fusion.29
  154.8 2.7 convert_element_type.84
  157.5 2.0 fusion.82
  159.5 1.4 convolution_multiply_fusion.3
  161.0 2.1 fusion.38
  163.1 1.4 fusion.39
  164.5 1.2 convolution_reduce_fusion.1
  165.7 123.4 %psum.15 = f32[1408]{0:T(1024)S(1)} all-reduce(f32[1408]{0:T(1024)S(1)} %add_multiply_fusion), channel_id=1, replica_groups=mesh['frame'=16,'crop'=4,'dp'=8] {'frame','crop'}, use_global_device_ids=true, to_apply=%region_16.17 | all-reduce | flops 1408 | bytes 11264 | tf_op jit(solution)/shard_map/psum | solution.py:116
  292.0 1.3 fusion.81
  294.2 20.8 %all-gather.6 = f32[16,1,256]{2,1,0:T(1,128)S(1)} all-gather(f32[1,1,256]{2,1,0:T(1,128)S(1)} %convolution_bitcast_fusion.6), channel_id=6, replica_groups=mesh['frame'=16,'crop'=4,'dp'=8] {'frame'}, dimensions={0}, use_global_device_ids=true | all-gather | bytes 17408 | tf_op jit(solution)/shard_map/all_gather | solution.py:15
  315.6 1.4 dynamic-update-slice.2
  316.9 1.4 dynamic-update-slice.3
  318.3 24.0 %all-reduce.13 = (f32[64]{0:T(128)S(1)}, f32[64]{0:T(128)S(1)}, f32[16]{0:T(128)}, f32[16]{0:T(128)}) all-reduce(f32[64]{0:T(128)S(1)} %dynamic-update-slice, f32[64]{0:T(128)S(1)} %dynamic-update-slice.1, f32[16]{0:T(128)S(1)} %dynamic-update-slice.2, f32[16]{0:T(128)S(1)} %dynamic-update-slice.3), channel_id=3, replica_groups=mesh['frame'=16,'crop'=4,'dp'=8] {'frame'}, use_global_device_ids=true, to_apply=%add.3 | all-reduce | flops 160 | bytes 1280
  344.1 86.0 %while.20 = (s32[]{:T(128)}, f32[4]{0:T(128)S(1)}, f32[4]{0:T(128)S(1)}, f32[4,256]{1,0:T(4,128)S(1)}, f32[]{:T(128)}, /*index=5*/f32[]{:T(128)}, f32[256]{0:T(2...) while((s32[]{:T(128)}, f32[4]{0:T(128)S(1)}, ...), condition=%wide.region_21.22_spmd, body=%wide.region_20.21_spmd.sunk | while | flops 3872 | bytes 17849 | solution.py:18
  432.0 2.0 fusion.36
  434.5 1.3 convolution_bitcast_fusion.1
  435.8 1.2 convolution_bitcast_fusion.2
  438.0 2.2 fusion.65
  440.1 2.5 fusion.75
  442.9 2.0 copy.54
  444.9 2.8 reshape.240
  447.8 5.8 copy.55
  453.6 1.9 fusion.59
  455.9 6.9 %convolution_bitcast_fusion = f32[1408,264]{1,0:T(8,128)} fusion(f32[16,64,264]{2,0,1:T(8,128)S(1)} %fusion.59, bf16[16,1,64,1408]{3,2,1,0:T(8,128)(2,1)S(1)} %copy-done.3, f32[16,64]{1,0:T(8,128)S(1)} %copy-done.27, f32[16,64]{1,0:T(8,128)S(1)} %copy-done.20), kind=kOutput, calls=%fused_computation.27 | convolution fusion | flops 4573364224 | bytes 5459968 | tf_op jit(solution)/shard_map/fpd,fpc->dc/dot_general | solution.py:161
  462.8 125.1 %fusion.79 = (f32[48,264]{1,0:T(8,128)S(1)}, f32[88,48]{0,1:T(8,128)S(1)}, f32[48,256]{1,0:T(8,128)S(1)}) fusion(f32[1408,264]{1,0:T(8,128)} %convolution_bitcast_fusion, f32[88,1408]{0,1:T(8,128)S(1)} %copy-done.7, f32[1408,256]{1,0:T(8,128)S(1)} %copy-done.6), kind=kCustom, calls=%all-reduce-scatter.3 | all-reduce-scatter fusion | flops 933889 | bytes 3543040
  587.8 1.9 collective-permute-start.4
  589.8 1.9 collective-permute-start.3
  591.7 1.9 collective-permute-start.5
  593.6 1.3 dynamic-slice.12
  595.6 11.1 %collective-permute-start.1 = (f32[48,264]{1,0:T(8,128)S(1)}, f32[48,264]{1,0:T(8,128)S(1)}, u32[]{:S(2)}, u32[]{:S(2)}) collective-permute-start(f32[48,264]{1,0:T(8,128)S(1)} %get-tuple-element.112), channel_id=1, source_target_pairs={{0,2},{1,3},{2,4},{3,5},{4,6},{5,7},{6,8},{7,9},{8,10},{9,11},{10,... | collective-permute-start | bytes 152072
  606.6 1.9 collective-permute-start
  608.6 2.5 collective-permute-start.7
  611.1 1.9 collective-permute-start.6
  613.0 2.3 collective-permute-start.8
  616.5 7.7 %collective-permute-done.8 = f32[28,256]{1,0:T(8,128)S(1)} collective-permute-done((f32[28,256]{1,0:T(8,128)S(1)}, f32[28,256]{1,0:T(8,128)S(1)}, u32[]{:S(2)}, u32[]{:S(2)}) %collective-permute-start.8) | collective-permute-done | bytes 28704
  624.1 1.9 collective-permute-start.2
  627.2 7.7 %collective-permute-done.2 = f32[28,264]{1,0:T(8,128)S(1)} collective-permute-done((f32[28,264]{1,0:T(8,128)S(1)}, f32[28,264]{1,0:T(8,128)S(1)}, u32[]{:S(2)}, u32[]{:S(2)}) %collective-permute-start.2) | collective-permute-done | bytes 29600
  (238 shorter events, 43.6 us)
Async XLA Ops:
  7.2 115.4 %copy-start = (bf16[256,2048]{1,0:T(8,128)(2,1)S(1)}, bf16[256,2048]{1,0:T(8,128)(2,1)}, u32[]{:S(2)}) copy-start(bf16[256,2048]{1,0:T(8,128)(2,1)} %param.20) | copy-start | bytes 3145732
  7.2 46.5 %all-gather.9.cloned.1.call-start = ((), (), s32[]{:S(2)}) async-start(), calls=%async_computation | async-start | bytes 3063808 | tf_op jit(solution)/shard_map/all_gather | solution.py:82
  53.7 3.4 copy-start.1
  57.1 1.5 copy-start.35
  57.1 0.9 copy-start.18
  58.0 0.6 copy-start.25
  68.3 7.5 %copy-start.4 = (bf16[8,256,1,3,88]{4,0,1,3,2:T(8,128)(2,1)}, bf16[8,256,1,3,88]{4,0,1,3,2:T(8,128)(2,1)S(1)}, u32[]{:S(2)}) copy-start(bf16[8,256,1,3,88]{4,0,1,3,2:T(8,128)(2,1)S(1)} %copy_select_fusion) | copy-start | bytes 3244036
  68.8 7.9 %copy-start.10 = (bf16[88,1408]{1,0:T(8,128)(2,1)S(1)}, bf16[88,1408]{1,0:T(8,128)(2,1)}, u32[]{:S(2)}) copy-start(bf16[88,1408]{1,0:T(8,128)(2,1)} %param.18) | copy-start | bytes 743428
  75.6 46.2 %copy-start.14 = (f32[16,1408]{1,0:T(8,128)S(1)}, f32[16,1408]{1,0:T(8,128)}, u32[]{:S(2)}) copy-start(f32[16,1408]{1,0:T(8,128)} %get-tuple-element.77) | copy-start | bytes 270340
  75.7 46.4 %copy-start.12 = (bf16[1408,256]{1,0:T(8,128)(2,1)S(1)}, bf16[1408,256]{1,0:T(8,128)(2,1)}, u32[]{:S(2)}) copy-start(bf16[1408,256]{1,0:T(8,128)(2,1)} %param.19) | copy-start | bytes 2162692
  75.8 0.8 copy-start.8
  76.6 74.2 %copy-start.19 = (f32[16,64]{1,0:T(8,128)S(1)}, f32[16,64]{1,0:T(8,128)}, u32[]{:S(2)}) copy-start(f32[16,64]{1,0:T(8,128)} %copy-done.18) | copy-start | bytes 12292
  76.6 74.2 %copy-start.26 = (f32[16,64]{1,0:T(8,128)S(1)}, f32[16,64]{1,0:T(8,128)}, u32[]{:S(2)}) copy-start(f32[16,64]{1,0:T(8,128)} %copy-done.25) | copy-start | bytes 12292
  76.7 73.6 %copy-start.23 = (f32[4,88]{1,0:T(4,128)}, f32[4,88]{1,0:T(4,128)S(1)}, u32[]{:S(2)}) copy-start(f32[4,88]{1,0:T(4,128)S(1)} %bitcast_reduce_fusion) | copy-start | bytes 4228
  121.9 29.0 %copy-start.2 = (bf16[16,1,64,1408]{3,2,1,0:T(8,128)(2,1)S(1)}, bf16[16,1,64,1408]{3,2,1,0:T(8,128)(2,1)}, u32[]{:S(2)}) copy-start(bf16[16,1,64,1408]{3,2,1,0:T(8,128)(2,1)} %all-gather.9.cloned.1.call-done) | copy-start | bytes 8650756
  122.6 2.4 copy-start.16
  122.6 0.7 copy-start.30
  123.3 27.0 %copy-start.28 = (f32[4]{0:T(128)}, f32[4]{0:T(128)S(1)}, u32[]{:S(2)}) copy-start(f32[4]{0:T(128)S(1)} %get-tuple-element.128) | copy-start | bytes 52
  150.2 0.6 copy-start.15
  159.5 6.2 copy-start.21
  159.5 129.6 %copy-start.11 = (bf16[1408,256]{1,0:T(8,128)(2,1)S(1)}, bf16[1408,256]{1,0:T(8,128)(2,1)}, u32[]{:S(2)}) copy-start(bf16[1408,256]{1,0:T(8,128)(2,1)} %param.16) | copy-start | bytes 2162692
  161.0 130.4 %copy-start.22 = (f32[2048]{0:T(1024)S(1)}, f32[2048]{0:T(1024)}, u32[]{:S(2)}) copy-start(f32[2048]{0:T(1024)} %param.21) | copy-start | bytes 24580
  163.1 152.0 %copy-start.29 = (f32[4]{0:T(128)S(1)}, f32[4]{0:T(128)}, u32[]{:S(2)}) copy-start(f32[4]{0:T(128)} %copy-done.28) | copy-start | bytes 52
  163.1 152.2 %copy-start.34 = (f32[4]{0:T(128)S(1)}, f32[4]{0:T(128)}, u32[]{:S(2)}) copy-start(f32[4]{0:T(128)} %fusion.56) | copy-start | bytes 52
  163.1 181.0 %slice-start = ((f32[16,4,256]{2,1,0:T(4,128)}), f32[15,4,256]{2,1,0:T(4,128)S(1)}, s32[]{:S(2)}) async-start(f32[16,4,256]{2,1,0:T(4,128)} %copy-done.15), calls=%async_computation.1 | async-start | bytes 122880 | tf_op jit(solution)/shard_map/slice | solution.py:17
  164.5 266.2 %copy-start.17 = (f32[4,256]{1,0:T(4,128)S(1)}, f32[4,256]{1,0:T(4,128)}, u32[]{:S(2)}) copy-start(f32[4,256]{1,0:T(4,128)} %copy-done.16) | copy-start | bytes 12292
  164.5 266.2 %copy-start.31 = (f32[4]{0:T(128)S(1)}, f32[4]{0:T(128)}, u32[]{:S(2)}) copy-start(f32[4]{0:T(128)} %copy-done.30) | copy-start | bytes 52
  289.5 141.4 %copy-start.13 = (bf16[1408,256]{1,0:T(8,128)(2,1)S(1)}, bf16[1408,256]{1,0:T(8,128)(2,1)}, u32[]{:S(2)}) copy-start(bf16[1408,256]{1,0:T(8,128)(2,1)} %param.19) | copy-start | bytes 2162692
  430.9 3.5 copy-start.5
  435.7 1.2 copy-start.9
  435.7 2.2 copy-start.24
  437.0 3.2 copy-start.32
  447.8 5.8 copy-start.33
  453.6 2.3 copy-start.3
  453.6 2.3 copy-start.20
  453.6 2.3 copy-start.27
  455.9 6.9 %copy-start.6 = (f32[1408,256]{1,0:T(8,128)S(1)}, f32[1408,256]{1,0:T(8,128)}, u32[]{:S(2)}) copy-start(f32[1408,256]{1,0:T(8,128)} %fusion.75) | copy-start | bytes 4325380
  455.9 6.9 %copy-start.7 = (f32[88,1408]{0,1:T(8,128)S(1)}, f32[88,1408]{0,1:T(8,128)}, u32[]{:S(2)}) copy-start(f32[88,1408]{0,1:T(8,128)} %fusion.65) | copy-start | bytes 1486852
  587.8 23.2 %collective-permute-start.4 = (f32[88,48]{0,1:T(8,128)S(1)}, f32[88,48]{0,1:T(8,128)S(1)}, u32[]{:S(2)}, u32[]{:S(2)}) collective-permute-start(f32[88,48]{0,1:T(8,128)S(1)} %get-tuple-element.113), channel_id=1, source_target_pairs={{0,2},{1,3},{2,4},{3,5},{4,6},{5,7},{6,8},{7,9},{8,10},{9,11},{10,... | collective-permute-start | bytes 50696
  589.8 23.3 %collective-permute-start.3 = (f32[88,48]{0,1:T(8,128)S(1)}, f32[88,48]{0,1:T(8,128)S(1)}, u32[]{:S(2)}, u32[]{:S(2)}) collective-permute-start(f32[88,48]{0,1:T(8,128)S(1)} %get-tuple-element.113), channel_id=1, source_target_pairs={{0,1},{1,2},{2,3},{3,4},{4,5},{5,6},{6,7},{7,8},{8,9},{9,10},{10,1... | collective-permute-start | bytes 50696
  591.7 16.9 %collective-permute-start.5 = (f32[88,28]{0,1:T(8,128)S(1)}, f32[88,28]{0,1:T(8,128)S(1)}, u32[]{:S(2)}, u32[]{:S(2)}) collective-permute-start(f32[88,28]{0,1:T(8,128)S(1)} %slice.100), channel_id=1, source_target_pairs={{0,3},{1,4},{2,5},{3,6},{4,7},{5,8},{6,9},{7,10},{8,11},{9,12},{10... | collective-permute-start | bytes 29576
  595.6 39.3 %collective-permute-start.1 = (f32[48,264]{1,0:T(8,128)S(1)}, f32[48,264]{1,0:T(8,128)S(1)}, u32[]{:S(2)}, u32[]{:S(2)}) collective-permute-start(f32[48,264]{1,0:T(8,128)S(1)} %get-tuple-element.112), channel_id=1, source_target_pairs={{0,2},{1,3},{2,4},{3,5},{4,6},{5,7},{6,8},{7,9},{8,10},{9,11},{10,... | collective-permute-start | bytes 152072
  606.6 28.3 %collective-permute-start = (f32[48,264]{1,0:T(8,128)S(1)}, f32[48,264]{1,0:T(8,128)S(1)}, u32[]{:S(2)}, u32[]{:S(2)}) collective-permute-start(f32[48,264]{1,0:T(8,128)S(1)} %get-tuple-element.112), channel_id=1, source_target_pairs={{0,1},{1,2},{2,3},{3,4},{4,5},{5,6},{6,7},{7,8},{8,9},{9,10},{10,1... | collective-permute-start | bytes 152072
  608.6 17.5 %collective-permute-start.7 = (f32[48,256]{1,0:T(8,128)S(1)}, f32[48,256]{1,0:T(8,128)S(1)}, u32[]{:S(2)}, u32[]{:S(2)}) collective-permute-start(f32[48,256]{1,0:T(8,128)S(1)} %get-tuple-element.114), channel_id=1, source_target_pairs={{0,2},{1,3},{2,4},{3,5},{4,6},{5,7},{6,8},{7,9},{8,10},{9,11},{10,... | collective-permute-start | bytes 147464
  611.1 15.0 %collective-permute-start.6 = (f32[48,256]{1,0:T(8,128)S(1)}, f32[48,256]{1,0:T(8,128)S(1)}, u32[]{:S(2)}, u32[]{:S(2)}) collective-permute-start(f32[48,256]{1,0:T(8,128)S(1)} %get-tuple-element.114), channel_id=1, source_target_pairs={{0,1},{1,2},{2,3},{3,4},{4,5},{5,6},{6,7},{7,8},{8,9},{9,10},{10,1... | collective-permute-start | bytes 147464
  613.0 11.1 %collective-permute-start.8 = (f32[28,256]{1,0:T(8,128)S(1)}, f32[28,256]{1,0:T(8,128)S(1)}, u32[]{:S(2)}, u32[]{:S(2)}) collective-permute-start(f32[28,256]{1,0:T(8,128)S(1)} %slice.101), channel_id=1, source_target_pairs={{0,3},{1,4},{2,5},{3,6},{4,7},{5,8},{6,9},{7,10},{8,11},{9,12},{10... | collective-permute-start | bytes 86024
  624.1 10.8 %collective-permute-start.2 = (f32[28,264]{1,0:T(8,128)S(1)}, f32[28,264]{1,0:T(8,128)S(1)}, u32[]{:S(2)}, u32[]{:S(2)}) collective-permute-start(f32[28,264]{1,0:T(8,128)S(1)} %slice.99), channel_id=1, source_target_pairs={{0,3},{1,4},{2,5},{3,6},{4,7},{5,8},{6,9},{7,10},{8,11},{9,12},{10... | collective-permute-start | bytes 88712
Sparse Core Ops, SparseCore 0:
  10.1 43.5 all-gather.8
where the time goes:
time: 645 us; the launch traced here: 643 us
  blocking collectives  363 us (56%)
  loops' own time  65.7 us (10%)
  waiting for transfers between devices  55.4 us (9%)
  local copies, waits for them, and re-layouts  54.8 us (8%)
  matrix products  34.9 us (5%)
  starting transfers between devices  27.4 us (4%)
  other arithmetic  24.6 us (4%)
  between operations  16.7 us (3%)
    unnamed x2, blocking collectives  149 us
    psum x1, blocking collectives, local(): t_pooled = lax.psum(t_partial, ('frame', 'crop'))  123 us
    another operation x1, loops' own time, combined_all(): lax.scan(lambda running, share: (join(running, share), None), head, tail)  65.7 us
    all_gather x2, blocking collectives, combined_all(): pieces = jax.tree.map(lambda part: lax.all_gather(part, axis), value)  46.1 us
    psum x1, blocking collectives, local(): s_summed = lax.psum(s_partial, 'frame')  45 us
    all_gather x1, waiting for transfers between devices, local(): gathered = lax.all_gather(tokens, 'frame', axis=0, tiled=True)  39.3 us
    unnamed x9, starting transfers between devices  27.4 us
    dynamic_slice x30, local copies, waits for them, and re-layouts, combined_all(): lax.scan(lambda running, share: (join(running, share), None), head, tail)  18.4 us
  transfers between devices with their start and end apart: 10, of which 3 were waited for; matrix products, arithmetic and copies ran while one was open for 1% of the time, Pallas kernels for 0%

commit v1 on v0

--- a/solution.py
+++ b/solution.py
@@ -113,7 +113,7 @@
         axis=1,
     )
     local_mean = jnp.dot(picks, frame_sums, precision=HIGH) / local_count
-    t_pooled = lax.psum(t_partial, ("frame", "crop"))
+    t_pooled = lax.psum(lax.psum(t_partial, "crop"), "frame")
     s_summed = lax.psum(s_partial, "frame")
     s_pooled = local_mean + s_summed
     protos = prototypes.astype(jnp.float32)

time: 645 us -> 520 us (0.81)
  the two profiles are of different devices: /device:TPU:26 before, /device:TPU:18 now
where the time goes in v1:
time: 520 us; the launch traced here: 518 us
  blocking collectives  242 us (47%)
  loops' own time  63.4 us (12%)
  waiting for transfers between devices  56.6 us (11%)
  local copies, waits for them, and re-layouts  52.4 us (10%)
  matrix products  35.4 us (7%)
  starting transfers between devices  30.9 us (6%)
  other arithmetic  21.6 us (4%)
  between operations  16.5 us (3%)
    unnamed x2, blocking collectives  145 us
    another operation x1, loops' own time, combined_all(): lax.scan(lambda running, share: (join(running, share), None), head, tail)  63.4 us
    psum x1, blocking collectives, local(): s_summed = lax.psum(s_partial, 'frame')  47.1 us
    all_gather x1, waiting for transfers between devices, local(): gathered = lax.all_gather(tokens, 'frame', axis=0, tiled=True)  41.3 us
    all_gather x2, blocking collectives, combined_all(): pieces = jax.tree.map(lambda part: lax.all_gather(part, axis), value)  38.8 us
    unnamed x9, starting transfers between devices  30.9 us
    dynamic_slice x30, local copies, waits for them, and re-layouts, combined_all(): lax.scan(lambda running, share: (join(running, share), None), head, tail)  17.8 us
    unnamed x10, waiting for transfers between devices  15.4 us
  transfers between devices with their start and end apart: 10, of which 3 were waited for; matrix products, arithmetic and copies ran while one was open for 2% of the time, Pallas kernels for 0%

profile of v1, /device:TPU:18, one launch (start us, length us, event | category | flops | bytes accessed | tf_op | source)
XLA Modules:
  0.0 518.4 jit_solution(5337795691190359406)
XLA Ops:
  8.8 1.3 dynamic-slice
  13.2 41.3 %all-gather.9.cloned.1.call-done = bf16[16,1,64,1408]{3,2,1,0:T(8,128)(2,1)} async-done(((bf16[1,1,64,1408]{3,2,1,0:T(8,128)(2,1)}), bf16[16,1,64,1408]{3,2,1,0:T(8,128)(2,1)}) %all-gather.9.cloned.1.call-update) | async-done | bytes 2883600 | tf_op jit(solution)/shard_map/all_gather | solution.py:82
  54.5 2.8 convert_reduce_fusion
  58.4 1.8 fusion.26
  60.2 1.9 gather_fusion
  62.2 4.5 reshape.311
  66.7 1.3 copy_select_fusion
  68.5 6.9 %fusion.83 = (f32[256,8]{1,0:T(8,128)S(1)}, f32[256,8,8]{1,2,0:T(8,128)S(1)}) fusion(f32[256,8,8]{1,2,0:T(8,128)S(1)} %convolution_multiply_fusion.2), kind=kOutput, calls=%fused_computation.133 | output fusion | flops 32775 | bytes 139264 | tf_op jit(solution)/shard_map/sub | solution.py:36
  76.4 2.7 fusion.29
  79.1 2.7 convert_element_type.84
  81.9 2.0 fusion.82
  85.5 1.4 fusion.39
  86.9 1.2 convolution_reduce_fusion.1
  88.1 10.6 %psum.22 = f32[1408]{0:T(1024)S(1)} all-reduce(f32[1408]{0:T(1024)S(1)} %add_multiply_fusion), channel_id=1, replica_groups=mesh['frame'=16,'crop'=4,'dp'=8] {'crop'}, use_global_device_ids=true, to_apply=%region_16.17 | all-reduce | flops 1408 | bytes 11264 | tf_op jit(solution)/shard_map/psum | solution.py:116
  99.0 47.1 %all-reduce.14 = (f32[4,1408]{1,0:T(4,128)S(1)}, f32[1408]{0:T(1024)S(1)}) all-reduce(f32[4,1408]{1,0:T(4,128)S(1)} %fusion.67, f32[1408]{0:T(1024)S(1)} %psum.22), channel_id=1, replica_groups=mesh['frame'=16,'crop'=4,'dp'=8] {'frame'}, use_global_device_ids=true, to_apply=%region_8.9 | all-reduce | flops 7040 | bytes 56320 | tf_op jit(solution)/shard_map/psum | solution.py:117
  146.2 1.6 multiply_reduce_fusion.1
  149.7 20.8 %all-gather.5 = f32[16,4,256]{2,1,0:T(4,128)S(1)} all-gather(f32[1,4,256]{2,1,0:T(4,128)S(1)} %convolution_bitcast_fusion.5), channel_id=5, replica_groups=mesh['frame'=16,'crop'=4,'dp'=8] {'frame'}, dimensions={0}, use_global_device_ids=true | all-gather | bytes 69632 | tf_op jit(solution)/shard_map/all_gather | solution.py:15
  173.3 1.3 fusion.81
  175.4 18.0 %all-gather.6 = f32[16,1,256]{2,1,0:T(1,128)S(1)} all-gather(f32[1,1,256]{2,1,0:T(1,128)S(1)} %convolution_bitcast_fusion.6), channel_id=6, replica_groups=mesh['frame'=16,'crop'=4,'dp'=8] {'frame'}, dimensions={0}, use_global_device_ids=true | all-gather | bytes 17408 | tf_op jit(solution)/shard_map/all_gather | solution.py:15
  193.9 1.3 dynamic-update-slice.2
  195.3 1.4 dynamic-update-slice.3
  196.7 24.9 %all-reduce.13 = (f32[64]{0:T(128)S(1)}, f32[64]{0:T(128)S(1)}, f32[16]{0:T(128)}, f32[16]{0:T(128)}) all-reduce(f32[64]{0:T(128)S(1)} %dynamic-update-slice, f32[64]{0:T(128)S(1)} %dynamic-update-slice.1, f32[16]{0:T(128)S(1)} %dynamic-update-slice.2, f32[16]{0:T(128)S(1)} %dynamic-update-slice.3), channel_id=3, replica_groups=mesh['frame'=16,'crop'=4,'dp'=8] {'frame'}, use_global_device_ids=true, to_apply=%add.3 | all-reduce | flops 160 | bytes 1280
  223.3 83.0 %while.20 = (s32[]{:T(128)}, f32[4]{0:T(128)S(1)}, f32[4]{0:T(128)S(1)}, f32[4,256]{1,0:T(4,128)S(1)}, f32[]{:T(128)}, /*index=5*/f32[]{:T(128)}, f32[256]{0:T(2...) while((s32[]{:T(128)}, f32[4]{0:T(128)S(1)}, ...), condition=%wide.region_22.23_spmd, body=%wide.region_21.22_spmd.sunk | while | flops 3872 | bytes 17849 | solution.py:18
  307.2 1.9 fusion.76
  309.5 2.0 fusion.36
  312.0 1.3 convolution_bitcast_fusion.1
  313.2 1.2 convolution_bitcast_fusion.2
  314.5 1.0 convolution_bitcast_fusion.3
  315.4 2.2 fusion.65
  317.6 2.5 fusion.75
  320.4 2.0 copy.54
  322.4 2.8 reshape.240
  325.2 5.8 %copy.55 = bf16[32,64,264]{2,0,1:T(8,128)(2,1)} copy(bf16[32,64,264]{1,0,2:T(8,128)(2,1)S(1)} %reshape.240) | data formatting | bytes 2162688 | tf_op jit(solution)/shard_map/reshape | solution.py:156
  331.0 1.9 fusion.59
  333.3 6.9 %convolution_bitcast_fusion = f32[1408,264]{1,0:T(8,128)} fusion(f32[16,64,264]{2,0,1:T(8,128)S(1)} %fusion.59, bf16[16,1,64,1408]{3,2,1,0:T(8,128)(2,1)S(1)} %copy-done.3, f32[16,64]{1,0:T(8,128)S(1)} %add_rsqrt_fusion, f32[16,64]{1,0:T(8,128)S(1)} %broadcast_multiply_fusion), kind=kOutput, calls=%fused_computation.27 | convolution fusion | flops 4573364224 | bytes 5459968 | tf_op jit(solution)/shard_map/fpd,fpc->dc/dot_general | solution.py:161
  340.2 120.3 %fusion.79 = (f32[48,264]{1,0:T(8,128)S(1)}, f32[88,48]{0,1:T(8,128)S(1)}, f32[48,256]{1,0:T(8,128)S(1)}) fusion(f32[1408,264]{1,0:T(8,128)} %convolution_bitcast_fusion, f32[88,1408]{0,1:T(8,128)S(1)} %copy-done.7, f32[1408,256]{1,0:T(8,128)S(1)} %copy-done.6), kind=kCustom, calls=%all-reduce-scatter.3 | all-reduce-scatter fusion | flops 933889 | bytes 3543040
  460.5 1.9 collective-permute-start.4
  462.4 4.3 collective-permute-start.3
  466.7 1.9 collective-permute-start.5
  468.7 1.3 dynamic-slice.12
  470.6 12.0 %collective-permute-start.1 = (f32[48,264]{1,0:T(8,128)S(1)}, f32[48,264]{1,0:T(8,128)S(1)}, u32[]{:S(2)}, u32[]{:S(2)}) collective-permute-start(f32[48,264]{1,0:T(8,128)S(1)} %get-tuple-element.114), channel_id=1, source_target_pairs={{0,2},{1,3},{2,4},{3,5},{4,6},{5,7},{6,8},{7,9},{8,10},{9,11},{10,... | collective-permute-start | bytes 152072
  482.6 1.9 collective-permute-start
  484.6 2.5 collective-permute-start.7
  487.1 1.9 collective-permute-start.6
  489.0 2.5 collective-permute-start.8
  492.6 7.0 %collective-permute-done.8 = f32[28,256]{1,0:T(8,128)S(1)} collective-permute-done((f32[28,256]{1,0:T(8,128)S(1)}, f32[28,256]{1,0:T(8,128)S(1)}, u32[]{:S(2)}, u32[]{:S(2)}) %collective-permute-start.8) | collective-permute-done | bytes 28704
  499.6 1.9 collective-permute-start.2
  502.7 7.7 %collective-permute-done.2 = f32[28,264]{1,0:T(8,128)S(1)} collective-permute-done((f32[28,264]{1,0:T(8,128)S(1)}, f32[28,264]{1,0:T(8,128)S(1)}, u32[]{:S(2)}, u32[]{:S(2)}) %collective-permute-start.2) | collective-permute-done | bytes 29600
  (195 shorter events, 41.2 us)
Async XLA Ops:
  7.2 140.7 %copy-start = (bf16[256,2048]{1,0:T(8,128)(2,1)S(1)}, bf16[256,2048]{1,0:T(8,128)(2,1)}, u32[]{:S(2)}) copy-start(bf16[256,2048]{1,0:T(8,128)(2,1)} %param.20) | copy-start | bytes 3145732
  7.2 47.3 %all-gather.9.cloned.1.call-start = ((), (), s32[]{:S(2)}) async-start(), calls=%async_computation | async-start | bytes 3063808 | tf_op jit(solution)/shard_map/all_gather | solution.py:82
  54.5 2.8 copy-start.1
  57.3 1.1 copy-start.13
  68.0 7.5 %copy-start.4 = (bf16[8,256,1,3,88]{4,0,1,3,2:T(8,128)(2,1)}, bf16[8,256,1,3,88]{4,0,1,3,2:T(8,128)(2,1)S(1)}, u32[]{:S(2)}) copy-start(bf16[8,256,1,3,88]{4,0,1,3,2:T(8,128)(2,1)S(1)} %copy_select_fusion) | copy-start | bytes 3244036
  68.5 7.9 %copy-start.2 = (bf16[16,1,64,1408]{3,2,1,0:T(8,128)(2,1)S(1)}, bf16[16,1,64,1408]{3,2,1,0:T(8,128)(2,1)}, u32[]{:S(2)}) copy-start(bf16[16,1,64,1408]{3,2,1,0:T(8,128)(2,1)} %all-gather.9.cloned.1.call-done) | copy-start | bytes 8650756
  68.5 7.9 %copy-start.14 = (bf16[1408,264]{0,1:T(8,128)(2,1)S(1)}, bf16[1408,264]{0,1:T(8,128)(2,1)}, u32[]{:S(2)}) copy-start(bf16[1408,264]{0,1:T(8,128)(2,1)} %param.14) | copy-start | bytes 2230276
  75.5 0.8 copy-start.8
  83.9 14.9 %copy-start.10 = (bf16[88,1408]{1,0:T(8,128)(2,1)S(1)}, bf16[88,1408]{1,0:T(8,128)(2,1)}, u32[]{:S(2)}) copy-start(bf16[88,1408]{1,0:T(8,128)(2,1)} %param.18) | copy-start | bytes 743428
  85.5 85.0 %copy-start.11 = (bf16[1408,256]{1,0:T(8,128)(2,1)S(1)}, bf16[1408,256]{1,0:T(8,128)(2,1)}, u32[]{:S(2)}) copy-start(bf16[1408,256]{1,0:T(8,128)(2,1)} %param.16) | copy-start | bytes 2162692
  147.8 24.8 %copy-start.12 = (f32[2048]{0:T(1024)S(1)}, f32[2048]{0:T(1024)}, u32[]{:S(2)}) copy-start(f32[2048]{0:T(1024)} %param.21) | copy-start | bytes 24580
  307.2 4.8 copy-start.5
  313.2 1.2 copy-start.9
  331.0 2.3 copy-start.3
  333.3 6.9 %copy-start.6 = (f32[1408,256]{1,0:T(8,128)S(1)}, f32[1408,256]{1,0:T(8,128)}, u32[]{:S(2)}) copy-start(f32[1408,256]{1,0:T(8,128)} %fusion.75) | copy-start | bytes 4325380
  333.3 6.9 %copy-start.7 = (f32[88,1408]{0,1:T(8,128)S(1)}, f32[88,1408]{0,1:T(8,128)}, u32[]{:S(2)}) copy-start(f32[88,1408]{0,1:T(8,128)} %fusion.65) | copy-start | bytes 1486852
  460.5 26.6 %collective-permute-start.4 = (f32[88,48]{0,1:T(8,128)S(1)}, f32[88,48]{0,1:T(8,128)S(1)}, u32[]{:S(2)}, u32[]{:S(2)}) collective-permute-start(f32[88,48]{0,1:T(8,128)S(1)} %get-tuple-element.115), channel_id=1, source_target_pairs={{0,2},{1,3},{2,4},{3,5},{4,6},{5,7},{6,8},{7,9},{8,10},{9,11},{10,... | collective-permute-start | bytes 50696
  462.4 26.6 %collective-permute-start.3 = (f32[88,48]{0,1:T(8,128)S(1)}, f32[88,48]{0,1:T(8,128)S(1)}, u32[]{:S(2)}, u32[]{:S(2)}) collective-permute-start(f32[88,48]{0,1:T(8,128)S(1)} %get-tuple-element.115), channel_id=1, source_target_pairs={{0,1},{1,2},{2,3},{3,4},{4,5},{5,6},{6,7},{7,8},{8,9},{9,10},{10,1... | collective-permute-start | bytes 50696
  466.7 17.8 %collective-permute-start.5 = (f32[88,28]{0,1:T(8,128)S(1)}, f32[88,28]{0,1:T(8,128)S(1)}, u32[]{:S(2)}, u32[]{:S(2)}) collective-permute-start(f32[88,28]{0,1:T(8,128)S(1)} %slice.100), channel_id=1, source_target_pairs={{0,3},{1,4},{2,5},{3,6},{4,7},{5,8},{6,9},{7,10},{8,11},{9,12},{10... | collective-permute-start | bytes 29576
  470.6 39.8 %collective-permute-start.1 = (f32[48,264]{1,0:T(8,128)S(1)}, f32[48,264]{1,0:T(8,128)S(1)}, u32[]{:S(2)}, u32[]{:S(2)}) collective-permute-start(f32[48,264]{1,0:T(8,128)S(1)} %get-tuple-element.114), channel_id=1, source_target_pairs={{0,2},{1,3},{2,4},{3,5},{4,6},{5,7},{6,8},{7,9},{8,10},{9,11},{10,... | collective-permute-start | bytes 152072
  482.6 27.8 %collective-permute-start = (f32[48,264]{1,0:T(8,128)S(1)}, f32[48,264]{1,0:T(8,128)S(1)}, u32[]{:S(2)}, u32[]{:S(2)}) collective-permute-start(f32[48,264]{1,0:T(8,128)S(1)} %get-tuple-element.114), channel_id=1, source_target_pairs={{0,1},{1,2},{2,3},{3,4},{4,5},{5,6},{6,7},{7,8},{8,9},{9,10},{10,1... | collective-permute-start | bytes 152072
  484.6 17.0 %collective-permute-start.7 = (f32[48,256]{1,0:T(8,128)S(1)}, f32[48,256]{1,0:T(8,128)S(1)}, u32[]{:S(2)}, u32[]{:S(2)}) collective-permute-start(f32[48,256]{1,0:T(8,128)S(1)} %get-tuple-element.116), channel_id=1, source_target_pairs={{0,2},{1,3},{2,4},{3,5},{4,6},{5,7},{6,8},{7,9},{8,10},{9,11},{10,... | collective-permute-start | bytes 147464
  487.1 14.5 %collective-permute-start.6 = (f32[48,256]{1,0:T(8,128)S(1)}, f32[48,256]{1,0:T(8,128)S(1)}, u32[]{:S(2)}, u32[]{:S(2)}) collective-permute-start(f32[48,256]{1,0:T(8,128)S(1)} %get-tuple-element.116), channel_id=1, source_target_pairs={{0,1},{1,2},{2,3},{3,4},{4,5},{5,6},{6,7},{7,8},{8,9},{9,10},{10,1... | collective-permute-start | bytes 147464
  489.0 10.6 %collective-permute-start.8 = (f32[28,256]{1,0:T(8,128)S(1)}, f32[28,256]{1,0:T(8,128)S(1)}, u32[]{:S(2)}, u32[]{:S(2)}) collective-permute-start(f32[28,256]{1,0:T(8,128)S(1)} %slice.101), channel_id=1, source_target_pairs={{0,3},{1,4},{2,5},{3,6},{4,7},{5,8},{6,9},{7,10},{8,11},{9,12},{10... | collective-permute-start | bytes 86024
  499.6 10.8 %collective-permute-start.2 = (f32[28,264]{1,0:T(8,128)S(1)}, f32[28,264]{1,0:T(8,128)S(1)}, u32[]{:S(2)}, u32[]{:S(2)}) collective-permute-start(f32[28,264]{1,0:T(8,128)S(1)} %slice.99), channel_id=1, source_target_pairs={{0,3},{1,4},{2,5},{3,6},{4,7},{5,8},{6,9},{7,10},{8,11},{9,12},{10... | collective-permute-start | bytes 88712
Sparse Core Ops, SparseCore 0:
  10.1 44.3 all-gather.8
